TPU v7x, 32 devices: a whole 2x2x4 slice. The times are simulated.
32 devices in a mesh: groups: 2 (over y), img: 4 (over z), tpl: 2 (over x), sub: 2 (over core).
Axes of the slice: x: 2, y: 2, z: 4, core: 2. Of those that a mesh axis runs over, the one named last changes fastest.
Arguments:
- images: bfloat16 [2048, 4096], P(('groups', 'img', 'tpl', 'sub')), parts along dimension 0, may hold values from -48 to 48
- templates: bfloat16 [4096, 4096], P(('groups', 'tpl', 'sub')), parts along dimension 0, may hold values from -1 to 1, as said below
- group_ids: int32 [2048], P(('groups', 'img')), parts along dimension 0, may hold values from 0 to 31
- group_ctf: float32 [64], P('groups'), parts along dimension 0, may hold values from 1 to 2
- group_prec: float32 [64], P('groups'), parts along dimension 0, may hold values from 1 to 3
- log_prior: float32 [256], P('groups'), parts along dimension 0, may hold values from -4.5 to 4.5
- class_mask: int32 [256], P('groups'), parts along dimension 0, may hold values from 0 to 1
Outputs:
- class_sums: float32 [4096, 4096], P(('groups', 'tpl', 'sub'), 'img'), parts along dimension 0
- evidence: float32 [2048], P(('groups', 'img', 'tpl', 'sub')), parts along dimension 0
There are 2 independent parts, one for each index of `groups`. A program takes and returns all parts, laid end to end along the dimension named above; each array names one. Nothing has to cross between parts.
Inputs may be any that keep to these rules, and one draw needn't show every extreme that they name: `templates`: each row has unit length before rounding.
All inputs are finite; a program needn't handle non-finite values.
Results may differ from a plain program's by a relative error of at most 0.0028.
Values may be sent and summed in bfloat16 or wider, within the bound.
A program may use at most 64 MiB of HBM per device.

v0:
```python
import jax
import jax.numpy as jnp
from jax import lax
from jax.sharding import PartitionSpec as P

ROTS = 16


masked_score = -1e30


def lookup(table, indices):
    columns = jnp.arange(table.shape[0], dtype=jnp.int32)
    return jnp.sum(jnp.where(indices[:, None] == columns[None, :], table[None, :], 0.0), axis=1)


def row_tables(log_prior, class_mask, first_class, class_count):
    prior_rows = jnp.repeat(lax.dynamic_slice_in_dim(log_prior, first_class, class_count), ROTS)
    active = jnp.repeat(lax.dynamic_slice_in_dim(class_mask, first_class, class_count), ROTS) > 0
    return (prior_rows, active)


def scored(raw_dots, tmpl_norm, scale_ctf, scale_prec, prior_rows, active):
    factor = (scale_prec * scale_ctf)[:, None]
    penalty = (0.5 * scale_prec * scale_ctf * scale_ctf)[:, None] * tmpl_norm[None, :]
    values = factor * raw_dots - penalty + prior_rows[None, :]
    return jnp.where(active[None, :], values, masked_score)


def posterior_rows(values, active):
    local_peak = jnp.max(values, axis=1)
    score_peak = lax.pmax(local_peak, ("tpl", "sub"))
    expo_terms = jnp.where(active[None, :], jnp.exp(values - score_peak[:, None]), 0.0)
    score_total = lax.psum(jnp.sum(expo_terms, axis=1), ("tpl", "sub"))
    return (expo_terms / score_total[:, None], score_peak + jnp.log(score_total))


def body(images, templates, group_ids, group_ctf, group_prec, log_prior, class_mask):
    rows_in = images.shape[0]
    local_refs = templates.shape[0]
    scale_ctf = lookup(group_ctf, group_ids)
    scale_prec = lookup(group_prec, group_ids)
    own_offset = lax.axis_index(("tpl", "sub")) * rows_in
    gathered = lax.all_gather(images, ("tpl", "sub"), axis=0, tiled=True)
    raw_dots = lax.dot_general(
        gathered, templates, (((1,), (1,)), ((), ())), preferred_element_type=jnp.float32
    )
    tmpl_norm = jnp.sum(jnp.square(templates.astype(jnp.float32)), axis=1)
    class_count = local_refs // ROTS
    prior_rows, active = row_tables(
        log_prior, class_mask, lax.axis_index(("tpl", "sub")) * class_count, class_count
    )
    values = scored(raw_dots, tmpl_norm, scale_ctf, scale_prec, prior_rows, active)
    posterior, evidence = posterior_rows(values, active)
    weight = (posterior * (scale_prec * scale_ctf)[:, None]).astype(jnp.bfloat16)
    totals = lax.psum_scatter(
        lax.dot_general(
            gathered, weight, (((0,), (0,)), ((), ())), preferred_element_type=jnp.float32
        ),
        "img",
        scatter_dimension=0,
        tiled=True,
    )
    class_sums = totals.T
    return (class_sums, lax.dynamic_slice_in_dim(evidence, own_offset, rows_in))


def solution(mesh):
    placed = (
        P(("groups", "img", "tpl", "sub"), None),
        P(("groups", "tpl", "sub"), None),
        P(("groups", "img")),
        P("groups"),
        P("groups"),
        P("groups"),
        P("groups"),
    )
    return jax.shard_map(
        body,
        mesh=mesh,
        in_specs=placed,
        out_specs=(P(("groups", "tpl", "sub"), "img"), P(("groups", "img", "tpl", "sub"))),
        check_vma=False,
    )
```

profile of v0, /device:TPU:1, one launch (start us, length us, event | category | flops | bytes accessed | tf_op | source)
XLA Modules:
  0.0 207.6 jit_solution(16777307062025537521)
XLA Ops:
  7.2 0.0 all-gather.2.cloned.1.call-start
  7.2 0.7 all-gather.2.cloned.1.call-update
  7.9 0.0 reduce-scatter.2.cloned.1.call-start
  7.9 0.7 dynamic_slice.10
  8.7 0.7 dynamic-slice_compare_fusion
  9.4 0.1 broadcast_in_dim.56
  9.5 0.1 gt.16
  9.6 0.1 broadcast_in_dim.61
  9.7 0.1 add.30
  9.7 0.8 select_reduce_fusion.1
  10.5 3.1 %multiply_reduce_fusion = f32[512]{0:T(512)S(1)} fusion(bf16[512,4096]{1,0:T(8,128)(2,1)} %param.8), kind=kLoop, calls=%fused_computation | loop fusion | flops 6290944 | bytes 4196352 | tf_op jit(solution)/shard_map/reduce_sum | solution.py:48
  13.6 21.0 %all-gather.2.cloned.1.call-done = bf16[256,4096]{1,0:T(8,128)(2,1)} async-done(((bf16[64,4096]{1,0:T(8,128)(2,1)}), bf16[256,4096]{1,0:T(8,128)(2,1)}) %all-gather.2.cloned.1.call-update) | async-done | bytes 2097168 | tf_op jit(solution)/shard_map/all_gather | solution.py:44
  34.6 0.0 copy-start
  34.6 4.4 %fusion.11 = (f32[256]{0:T(256)S(1)}, f32[256,512]{1,0:T(8,128)S(1)}) fusion(f32[512]{0:T(512)S(1)} %add.30, f32[512]{0:T(512)S(1)} %multiply_reduce_fusion, f32[256]{0:T(256)S(1)} %get-tuple-element.5, bf16[256,4096]{1,0:T(8,128)(2,1)} %all-gather.2.cloned.1.call-done, bf16[512,4096]{1,0:T(8,128)(2,1)} %param.8, f32[256]{0:T(256)S(1)} %get-tuple-element.4, ...), kind=kOutput, calls=%fused_computation.22 | convolution fusion | flops 1074528000 | bytes 6823424 | tf_op jit(solution)/shard_map/dot_general | solution.py:45
  38.9 5.3 %pmax.7 = f32[256]{0:T(256)S(1)} all-reduce(f32[256]{0:T(256)S(1)} %get-tuple-element.6), channel_id=1, replica_groups=mesh['groups'=2,'img'=4,'tpl'=2,'sub'=2] {'tpl','sub'}, use_global_device_ids=true, to_apply=%region_4.5 | all-reduce | flops 256 | bytes 2048 | tf_op jit(solution)/shard_map/pmax | solution.py:32
  44.2 0.2 fusion.3
  44.5 5.9 %psum.7 = f32[256]{0:T(256)S(1)} all-reduce(f32[256]{0:T(256)S(1)} %fusion.3), channel_id=1, replica_groups=mesh['groups'=2,'img'=4,'tpl'=2,'sub'=2] {'tpl','sub'}, use_global_device_ids=true, to_apply=%region_6.7 | all-reduce | flops 256 | bytes 2048 | tf_op jit(solution)/shard_map/psum | solution.py:34
  50.4 0.0 copy-done
  50.4 4.7 %convolution_bitcast_fusion = f32[4096,512]{0,1:T(8,128)} fusion(bf16[256,4096]{1,0:T(8,128)(2,1)S(1)} %copy-done, f32[256,512]{1,0:T(8,128)S(1)} %get-tuple-element.7, f32[256]{0:T(256)S(1)} %psum.7, f32[256]{0:T(256)S(1)} %pmax.7, f32[256]{0:T(256)S(1)} %get-tuple-element.4, pred[512]{0:T(512)(128)(4,1)S(1)} %gt.16), kind=kOutput, calls=%fused_computation.1 | convolution fusion | flops 1074397184 | bytes 11013632 | tf_op jit(solution)/shard_map/dot_general | solution.py:57
  55.0 0.0 reduce-scatter.2.cloned.1.call-update
  55.1 0.6 dynamic_slice.11
  55.7 145.1 %reduce-scatter.2.cloned.1.call-done = f32[1024,512]{0,1:T(8,128)} async-done(((f32[4096,512]{0,1:T(8,128)}), f32[1024,512]{0,1:T(8,128)}) %reduce-scatter.2.cloned.1.call-update) | async-done | bytes 2097168 | tf_op jit(solution)/shard_map/reduce_scatter | solution.py:56
  (2 shorter events, 0.0 us)
Async XLA Ops:
  7.2 27.4 %all-gather.2.cloned.1.call-start = ((), (), s32[]{:S(2)}) async-start(), calls=%async_computation.1 | async-start | bytes 2621440 | tf_op jit(solution)/shard_map/all_gather | solution.py:44
  7.9 192.8 %reduce-scatter.2.cloned.1.call-start = ((), (), s32[]{:S(2)}) async-start(), calls=%async_computation.2 | async-start | bytes 10485760 | tf_op jit(solution)/shard_map/reduce_scatter | solution.py:56
  34.6 15.8 %copy-start = (bf16[256,4096]{1,0:T(8,128)(2,1)S(1)}, bf16[256,4096]{1,0:T(8,128)(2,1)}, u32[]{:S(2)}) copy-start(bf16[256,4096]{1,0:T(8,128)(2,1)} %all-gather.2.cloned.1.call-done) | copy-start | bytes 6291460
Sparse Core Ops, SparseCore 0:
  9.5 25.0 all-gather.1
  55.2 145.4 reduce-scatter.1
where the time goes:
time: 209 us; the launch traced here: 208 us
  waiting for transfers between devices  167 us (80%)
  between operations  14.1 us (7%)
  blocking collectives  11.2 us (5%)
  matrix products  9.04 us (4%)
  other arithmetic  4.85 us (2%)
    reduce_scatter x1, waiting for transfers between devices, body(): lax.psum_scatter(lax.dot_general(gathered, weight, (((0,), (0,)), ((), ()...  145 us
    all_gather x1, waiting for transfers between devices, body(): gathered = lax.all_gather(images, ('tpl', 'sub'), axis=0, tiled=True)  21 us
    psum x1, blocking collectives, posterior_rows(): score_total = lax.psum(jnp.sum(expo_terms, axis=1), ('tpl', 'sub'))  5.89 us
    pmax x1, blocking collectives, posterior_rows(): score_peak = lax.pmax(local_peak, ('tpl', 'sub'))  5.29 us
    dot_general x1, matrix products, body(): lax.dot_general(gathered, weight, (((0,), (0,)), ((), ())), preferred_ele...  4.68 us
    dot_general x1, matrix products, body(): lax.dot_general(gathered, templates, (((1,), (1,)), ((), ())), preferred_...  4.36 us
  transfers between devices with their start and end apart: 2, of which 2 were waited for; matrix products, arithmetic and copies ran while one was open for 3% of the time, Pallas kernels for 0%

commit v1 on v0

v1 whole, which is shorter than its diff:
```python
import functools
import jax
import jax.numpy as jnp
from jax import lax
from jax.experimental import pallas as pl
from jax.experimental.pallas import tpu as pltpu
from jax.sharding import PartitionSpec as P

ROTS = 16
MASKED = -1e30
CHUNKS = 2
MESH = pl.DeviceIdType.MESH


def exchange_kernel(
    sizes, ids_ref, ctf_ref, prec_ref, prior_ref, mask_ref, images, templates,
    all_w, all_p, evid_ref,
    grid_buf, tmpl, tnorm, base, act, score, w_send, own_stat, stat,
    tmpl_sem, own_sem, a_send, a_recv, f_send, b_send, b_recv, g_send, s_send, s_recv,
    w_own, w_out, w_recv, p_own,
):
    Z, X, C, K, pb = sizes
    S = X * C
    g, z, x, c = [lax.axis_index(n) for n in ("groups", "img", "tpl", "sub")]
    s = x * C + c
    refs, nb = tnorm.shape
    classes = refs // ROTS

    def xc(dx, dc):
        return lax.rem(x + dx, X), lax.rem(c + dc, C)

    def dev(zz, xx, cc):
        return (g, zz, xx, cc)

    def zoff(d):
        return lax.rem(z + d, Z)

    peers = [(dx, dc) for dx in range(X) for dc in range(C) if dx or dc]

    barrier = pltpu.get_barrier_semaphore()
    for dx, dc in peers:
        pl.semaphore_signal(barrier, inc=1, device_id=dev(z, *xc(dx, dc)), device_id_type=MESH)
    for d in range(1, Z):
        pl.semaphore_signal(barrier, inc=1, device_id=dev(zoff(d), x, c), device_id_type=MESH)

    started = []

    def local(src, dst, sem):
        cp = pltpu.make_async_copy(src, dst, sem)
        cp.start()
        return cp

    def remote(src, dst, send, recv, to):
        cp = pltpu.make_async_remote_copy(
            src_ref=src, dst_ref=dst, send_sem=send, recv_sem=recv, device_id=to, device_id_type=MESH
        )
        cp.start()
        started.append(cp)

    def arrive(dst, sem):
        pltpu.make_async_copy(dst, dst, sem).wait()

    tmpl_copy = local(templates, tmpl, tmpl_sem)
    own_copies = [local(images.at[k], grid_buf.at[k, s], own_sem.at[k]) for k in range(K)]

    pl.semaphore_wait(barrier, S - 1 + Z - 1)

    def send_a(k):
        for dx in range(1, X):
            xx, cc = xc(dx, 0)
            remote(images.at[k], grid_buf.at[k, s], a_send.at[k, dx - 1], a_recv.at[k, s], dev(z, xx, cc))
        for dc in range(1, C):
            xx, cc = xc(0, dc)
            remote(images.at[k], grid_buf.at[k, s], a_send.at[k, X - 1 + dc - 1], a_recv.at[k, s], dev(z, xx, cc))

    send_a(0)
    for d in range(1, Z):
        zz = zoff(d)
        cols = pl.ds(pl.multiple_of(zz * pb, pb), pb)
        remote(images.at[:, :, cols], all_p.at[:, z, s], b_send.at[d - 1], b_recv.at[z, s], dev(zz, x, c))
    for k in range(1, K):
        send_a(k)

    first = s * classes
    for i in range(classes):
        rows = pl.ds(i * ROTS, ROTS)
        base[rows, :] = jnp.full((ROTS, nb), prior_ref[first + i], jnp.float32)
        act[rows, :] = jnp.full((ROTS, nb), mask_ref[first + i], jnp.int32).astype(jnp.float32)

    tmpl_copy.wait()

    @pl.loop(0, refs // 16)
    def _(i):
        rows = pl.ds(pl.multiple_of(i * 16, 16), 16)
        t = tmpl[rows, :].astype(jnp.float32)
        tnorm[rows, :] = jnp.broadcast_to(jnp.sum(t * t, axis=1, keepdims=True), (16, nb))

    def scales(k):
        ids = ids_ref[k]
        ctf = jnp.zeros_like(ids, dtype=jnp.float32)
        prec = ctf
        for i in range(ctf_ref.shape[0]):
            hit = ids == i
            ctf = jnp.where(hit, ctf_ref[i], ctf)
            prec = jnp.where(hit, prec_ref[i], prec)
        return ctf, prec

    p_copies = []

    def gather(k):
        own_copies[k].wait()
        for dx in range(1, X):
            xx, _ = xc(dx, 0)
            slot = xx * C + c
            arrive(grid_buf.at[k, slot], a_recv.at[k, slot])
            for dc in range(1, C):
                _, cc = xc(0, dc)
                remote(grid_buf.at[k, slot], grid_buf.at[k, slot], f_send.at[k, dx - 1, dc - 1], a_recv.at[k, slot], dev(z, x, cc))
        for dx in range(X):
            for dc in range(1, C):
                xx, cc = xc(dx, dc)
                slot = xx * C + cc
                arrive(grid_buf.at[k, slot], a_recv.at[k, slot])

    def scores(k):
        pix = grid_buf[k].reshape(nb, grid_buf.shape[3])
        raw = lax.dot_general(tmpl[...], pix, (((1,), (1,)), ((), ())), preferred_element_type=jnp.float32)
        ctf, prec = scales(k)
        values = (prec * ctf) * raw - (0.5 * prec * ctf * ctf) * tnorm[...] + base[...]
        values = jnp.where(act[...] > 0.0, values, MASKED)
        score[k] = values
        peak = jnp.max(values, axis=0, keepdims=True)
        total = jnp.sum(jnp.where(act[...] > 0.0, jnp.exp(values - peak), 0.0), axis=0, keepdims=True)
        row = lax.broadcasted_iota(jnp.int32, (8, nb), 0)
        own_stat[k] = jnp.where(row == 0, peak, total)
        for i, (dx, dc) in enumerate(peers):
            xx, cc = xc(dx, dc)
            remote(own_stat.at[k], stat.at[k, s], s_send.at[k, i], s_recv.at[k, s], dev(z, xx, cc))
        cols = pl.ds(pl.multiple_of(z * pb, pb), pb)
        p_copies.append(local(grid_buf.at[k, :, :, cols], all_p.at[k, z], p_own.at[k]))

    def w_block(ref, k, zz):
        return ref.at[:, pl.ds(pl.multiple_of((k * Z + zz) * nb, nb), nb)]

    def w_go(src, k, zz, right):
        step = 1 if right else -1
        return pltpu.make_async_remote_copy(
            src_ref=src, dst_ref=w_block(all_w, k, zz), send_sem=w_out.at[0 if right else 1, k, zz],
            recv_sem=w_recv.at[k, zz], device_id=dev(lax.rem(z + step + Z, Z), x, c), device_id_type=MESH,
        )

    w_copies = []

    def weights(k):
        parts = [(own_stat[k][0:1], own_stat[k][1:2])]
        for dx, dc in peers:
            xx, cc = xc(dx, dc)
            slot = xx * C + cc
            arrive(stat.at[k, slot], s_recv.at[k, slot])
            got = stat[k, slot]
            parts.append((got[0:1], got[1:2]))
        peak = functools.reduce(jnp.maximum, [p for p, _ in parts])
        total = functools.reduce(jnp.add, [t * jnp.exp(p - peak) for p, t in parts])
        evid_ref[k] = peak + jnp.log(total)
        ctf, prec = scales(k)
        post = jnp.where(act[...] > 0.0, jnp.exp(score[k] - peak), 0.0) / total
        w_send[k] = (post * (prec * ctf)).astype(jnp.bfloat16)

        @pl.when(z < Z - 1)
        def _():
            w_go(w_send.at[k], k, z, True).start()

        @pl.when(z > 0)
        def _():
            w_go(w_send.at[k], k, z, False).start()

        w_copies.append(local(w_send.at[k], w_block(all_w, k, z), w_own.at[k]))

    gather(0)
    scores(0)
    for k in range(1, K):
        gather(k)
        weights(k - 1)
        scores(k)
    weights(K - 1)

    for d in range(1, Z):
        zz = zoff(d)
        blk = all_p.at[:, zz, s]
        arrive(blk, b_recv.at[zz, s])
        for dx in range(1, X):
            xx, cc = xc(dx, 0)
            remote(blk, blk, g_send.at[d - 1, dx - 1, 0], b_recv.at[zz, s], dev(z, xx, cc))
        for dc in range(1, C):
            xx, cc = xc(0, dc)
            remote(blk, blk, g_send.at[d - 1, X - 1, dc - 1], b_recv.at[zz, s], dev(z, xx, cc))

    for d in range(1, Z):
        for k in range(K):
            @pl.when(z - d >= 0)
            def _():
                src = z - d
                arrive(w_block(all_w, k, src), w_recv.at[k, src])

                @pl.when(z < Z - 1)
                def _():
                    w_go(w_block(all_w, k, src), k, src, True).start()

            @pl.when(z + d < Z)
            def _():
                src = z + d
                arrive(w_block(all_w, k, src), w_recv.at[k, src])

                @pl.when(z > 0)
                def _():
                    w_go(w_block(all_w, k, src), k, src, False).start()
        zz = zoff(d)
        for dx in range(1, X):
            xx, _ = xc(dx, 0)
            blk = all_p.at[:, zz, xx * C + c]
            arrive(blk, b_recv.at[zz, xx * C + c])
            for dc in range(1, C):
                _, cc = xc(0, dc)
                remote(blk, blk, g_send.at[d - 1, dx - 1, dc], b_recv.at[zz, xx * C + c], dev(z, x, cc))

    for d in range(1, Z):
        zz = zoff(d)
        for dx in range(X):
            for dc in range(1, C):
                xx, cc = xc(dx, dc)
                arrive(all_p.at[:, zz, xx * C + cc], b_recv.at[zz, xx * C + cc])
    for cp in started:
        cp.wait_send()
    for k in range(K):
        w_copies[k].wait()
        p_copies[k].wait()
        for d in range(Z):
            @pl.when((z - d >= 0) & (z < Z - 1))
            def _():
                w_go(w_send.at[k], k, z - d, True).wait_send()

            @pl.when((z + d < Z) & (z > 0))
            def _():
                w_go(w_send.at[k], k, z + d, False).wait_send()


def exchange(mesh, images, templates, group_ids, group_ctf, group_prec, log_prior, class_mask):
    Z, X, C, K = mesh.shape["img"], mesh.shape["tpl"], mesh.shape["sub"], CHUNKS
    S = X * C
    rows, pix = images.shape
    refs = templates.shape[0]
    r = rows // K
    nb = S * r
    pb = pix // Z
    ids = group_ids.reshape(S, K, r).transpose(1, 0, 2).reshape(K, 1, nb)
    smem = pl.BlockSpec(memory_space=pltpu.SMEM)
    vmem = pl.BlockSpec(memory_space=pltpu.VMEM)
    anyw = pl.BlockSpec(memory_space=pl.ANY)
    dma = pltpu.SemaphoreType.DMA
    f32, bf16 = jnp.float32, jnp.bfloat16
    all_w, all_p, evid = pl.pallas_call(
        functools.partial(exchange_kernel, (Z, X, C, K, pb)),
        out_shape=(
            jax.ShapeDtypeStruct((refs, K * Z * nb), bf16),
            jax.ShapeDtypeStruct((K, Z, S, r, pb), bf16),
            jax.ShapeDtypeStruct((K, 1, nb), f32),
        ),
        in_specs=[vmem, smem, smem, smem, smem, anyw, anyw],
        out_specs=(anyw, anyw, vmem),
        scratch_shapes=[
            pltpu.VMEM((K, S, r, pix), bf16),
            pltpu.VMEM((refs, pix), bf16),
            pltpu.VMEM((refs, nb), f32),
            pltpu.VMEM((refs, nb), f32),
            pltpu.VMEM((refs, nb), f32),
            pltpu.VMEM((K, refs, nb), f32),
            pltpu.VMEM((K, refs, nb), bf16),
            pltpu.VMEM((K, 8, nb), f32),
            pltpu.VMEM((K, S, 8, nb), f32),
            dma(()), dma((K,)), dma((K, S)), dma((K, S)), dma((K, max(X - 1, 1), max(C - 1, 1))),
            dma((max(Z - 1, 1),)), dma((Z, S)), dma((max(Z - 1, 1), X, C)), dma((K, max(S - 1, 1))), dma((K, S)),
            dma((K,)), dma((2, K, Z)), dma((K, Z)), dma((K,)),
        ],
        compiler_params=pltpu.CompilerParams(
            collective_id=0, has_side_effects=True, vmem_limit_bytes=56 * 1024 * 1024
        ),
    )(ids, group_ctf, group_prec, log_prior, class_mask, images.reshape(K, r, pix), templates)
    class_sums = lax.dot_general(
        all_w, all_p.reshape(K * Z * nb, pb), (((1,), (0,)), ((), ())), preferred_element_type=f32
    )
    slot = lax.axis_index(("tpl", "sub"))
    own = lax.dynamic_slice_in_dim(evid.reshape(K, S, r), slot, 1, axis=1)
    return class_sums, own.reshape(rows)


def solution(mesh):
    placed = (
        P(("groups", "img", "tpl", "sub"), None),
        P(("groups", "tpl", "sub"), None),
        P(("groups", "img")),
        P("groups"),
        P("groups"),
        P("groups"),
        P("groups"),
    )
    return jax.shard_map(
        functools.partial(exchange, mesh),
        mesh=mesh,
        in_specs=placed,
        out_specs=(P(("groups", "tpl", "sub"), "img"), P(("groups", "img", "tpl", "sub"))),
        check_vma=False,
    )
```

time: 209 us -> 53.8 us (0.26)
  waiting for transfers between devices: 167 us -> 0 us
  Pallas kernels: 0 us -> 44.4 us
  between operations: 14.1 us -> 0.65 us
  blocking collectives: 11.2 us -> 0 us
  matrix products: 9.04 us -> 4.49 us
  other arithmetic: 4.85 us -> 1.33 us
    reduce_scatter x1 -> x0, waiting for transfers between devices: 145 us -> none  [body(): lax.psum_scatter(lax.dot_general(gathered, weight, (((0,), (0,)), ((), ()...]
    pallas_call x0 -> x1, Pallas kernels: none -> 44.4 us  [exchange(): pl.pallas_call(functools.partial(exchange_kernel, (Z, X, C, K, pb)), out_...]
    all_gather x1 -> x0, waiting for transfers between devices: 21 us -> none  [body(): gathered = lax.all_gather(images, ('tpl', 'sub'), axis=0, tiled=True)]
    psum x1 -> x0, blocking collectives: 5.89 us -> none  [posterior_rows(): score_total = lax.psum(jnp.sum(expo_terms, axis=1), ('tpl', 'sub'))]
    pmax x1 -> x0, blocking collectives: 5.29 us -> none  [posterior_rows(): score_peak = lax.pmax(local_peak, ('tpl', 'sub'))]
    dot_general x2 -> x1, matrix products: 9.04 us -> 4.49 us  [exchange(): lax.dot_general(all_w, all_p.reshape(K * Z * nb, pb), (((1,), (0,)), ((),...]
    reduce_sum x3 -> x0, other arithmetic: 4.1 us -> none  [the longest x1 3.08 us: body(): tmpl_norm = jnp.sum(jnp.square(templates.astype(jnp.float32)), axis=1)]
  transfers between devices with their start and end apart: 2 -> 0, of which waited for: 2 -> 0; matrix products, arithmetic and copies ran while one was open for 3% -> 0% of each run, Pallas kernels for 0% -> 0%
where the time goes in v1:
time: 53.8 us; the launch traced here: 53.5 us
  Pallas kernels  44.4 us (83%)
  matrix products  4.49 us (8%)
  local copies, waits for them, and re-layouts  2.62 us (5%)
  other arithmetic  1.33 us (2%)
  between operations  0.65 us (1%)
    pallas_call x1, Pallas kernels, exchange(): pl.pallas_call(functools.partial(exchange_kernel, (Z, X, C, K, pb)), out_...  44.4 us
    dot_general x1, matrix products, exchange(): lax.dot_general(all_w, all_p.reshape(K * Z * nb, pb), (((1,), (0,)), ((),...  4.49 us
    reshape x2, local copies, waits for them, and re-layouts, exchange(): ids = group_ids.reshape(S, K, r).transpose(1, 0, 2).reshape(K, 1, nb)  1.41 us
    pallas_call x1, other arithmetic, exchange(): pl.pallas_call(functools.partial(exchange_kernel, (Z, X, C, K, pb)), out_...  1.33 us

profile of v1, /device:TPU:1, one launch (start us, length us, event | category | flops | bytes accessed | tf_op | source)
XLA Modules:
  0.0 53.5 jit_solution(17514536533484633664)
XLA Ops:
  0.6 0.8 %reshape.22 = s32[4,2,32]{2,1,0:T(2,128)S(1)} reshape(s32[256]{0:T(256)} %param.9) | data formatting | bytes 2048 | tf_op jit(solution)/shard_map/reshape | solution.py:255
  1.4 0.6 %reshape.23.ids_ref = s32[2,1,128]{2,1,0:T(1,128)} reshape(s32[2,4,32]{2,1,0:T(4,128)S(1)} %copy.10) | data formatting | bytes 2048 | tf_op jit(solution)/shard_map/reshape | solution.py:255
  2.1 44.4 %shard_map.86 = (bf16[512,1024]{1,0:T(8,128)(2,1)}, bf16[2,4,4,32,1024]{4,3,2,1,0:T(8,128)(2,1)}, f32[2,1,128]{2,1,0:T(1,128)}) custom-call(s32[2,1,128]{2,1,0:T(1,128)} %reshape.23.ids_ref, f32[32]{0:T(128)} %ctf_ref.1, f32[32]{0:T(128)} %prec_ref.1, f32[128]{0:T(128)} %prior_ref.1, s32[128]{0:T(128)} %mask_ref.1, bf16[2,32,4096]{2,1,0:T(8,128)(2,1)} %bitcast.8, ...), custom_call_target="tpu_custom_call" | custom-call | tf_op jit(solution)/shard_map/pallas_call | solution.py:261
  46.5 0.5 broadcast.3
  47.0 1.3 %reduce.3 = f32[2,128]{1,0:T(2,128)S(1)} reduce(f32[2,1,128]{2,1,0:T(1,128)} %get-tuple-element.7, f32[]{:T(128)} %broadcast.3), dimensions={1}, to_apply=%get-tuple-element.7.reduce_sub_computation.3 | reduce | bytes 2052 | tf_op jit(solution)/shard_map/pallas_call | solution.py:261
  48.3 0.1 reshape.26
  48.4 0.6 %reshape.27 = f32[64]{0:T(128)} reshape(f32[2,1,32]{2,0,1:T(2,128)S(1)} %bitcast.10) | data formatting | bytes 512 | tf_op jit(solution)/shard_map/reshape | solution.py:293
  49.0 4.5 %fusion = f32[512,1024]{1,0:T(8,128)} fusion(bf16[512,1024]{1,0:T(8,128)(2,1)} %get-tuple-element.5, bf16[1024,1024]{1,0:T(8,128)(2,1)} %bitcast.11), kind=kOutput, calls=%fused_computation.1 | convolution fusion | flops 1073741824 | bytes 5242880 | tf_op jit(solution)/shard_map/dot_general | solution.py:288
  (2 shorter events, 0.0 us)

commit v2 on v1

v2 whole, which is shorter than its diff:
```python
import functools
import jax
import jax.numpy as jnp
from jax import lax
from jax.experimental import pallas as pl
from jax.experimental.pallas import tpu as pltpu
from jax.sharding import PartitionSpec as P

ROTS = 16
MASKED = -1e30
CHUNKS = 2
MESH = pl.DeviceIdType.MESH


def exchange_kernel(
    sizes, ids_ref, ctf_ref, prec_ref, prior_ref, mask_ref, images, templates,
    sums_ref, evid_ref,
    grid_buf, tmpl, tnorm, base, act, score, all_w, all_p, own_stat, stat,
    tmpl_sem, own_sem, a_send, a_recv, f_send, b_send, b_recv, g_send, s_send, s_recv,
    w_out, w_recv, p_own,
):
    Z, X, C, K, H = sizes
    S = X * C
    g, z, x, c = [lax.axis_index(n) for n in ("groups", "img", "tpl", "sub")]
    s = x * C + c
    refs, nb = tnorm.shape
    classes = refs // ROTS
    r, pix = grid_buf.shape[2:]
    pb = pix // Z
    h_rows = r // H

    def xc(dx, dc):
        return lax.rem(x + dx, X), lax.rem(c + dc, C)

    def dev(zz, xx, cc):
        return (g, zz, xx, cc)

    def zoff(d):
        return lax.rem(z + d, Z)

    peers = [(dx, dc) for dx in range(X) for dc in range(C) if dx or dc]

    barrier = pltpu.get_barrier_semaphore()
    for dx, dc in peers:
        pl.semaphore_signal(barrier, inc=1, device_id=dev(z, *xc(dx, dc)), device_id_type=MESH)
    for d in range(1, Z):
        pl.semaphore_signal(barrier, inc=1, device_id=dev(zoff(d), x, c), device_id_type=MESH)

    started = []

    def local(src, dst, sem):
        cp = pltpu.make_async_copy(src, dst, sem)
        cp.start()
        return cp

    def remote(src, dst, send, recv, to):
        cp = pltpu.make_async_remote_copy(
            src_ref=src, dst_ref=dst, send_sem=send, recv_sem=recv, device_id=to, device_id_type=MESH
        )
        cp.start()
        started.append(cp)

    def arrive(dst, sem):
        pltpu.make_async_copy(dst, dst, sem).wait()

    tmpl_copy = local(templates, tmpl, tmpl_sem)
    own_copies = [local(images.at[k], grid_buf.at[k, s], own_sem.at[k]) for k in range(K)]

    pl.semaphore_wait(barrier, S - 1 + Z - 1)

    def piece(k, h, slot):
        return grid_buf.at[k, slot, pl.ds(h * h_rows, h_rows), :]

    def send_a(k, h):
        src = images.at[k, pl.ds(h * h_rows, h_rows), :]
        for dx in range(1, X):
            xx, cc = xc(dx, 0)
            remote(src, piece(k, h, s), a_send.at[k, h, dx - 1], a_recv.at[k, h, s], dev(z, xx, cc))
        for dc in range(1, C):
            xx, cc = xc(0, dc)
            remote(src, piece(k, h, s), a_send.at[k, h, X - 1 + dc - 1], a_recv.at[k, h, s], dev(z, xx, cc))

    order = [(k, h) for k in range(K) for h in range(H)]
    early = [kh for kh in order if kh[0] == 0 or kh[1] < H - 1]
    for k, h in early[:H]:
        send_a(k, h)
    for d in range(1, Z):
        zz = zoff(d)
        cols = pl.ds(pl.multiple_of(zz * pb, pb), pb)
        remote(images.at[:, :, cols], all_p.at[z, :, s], b_send.at[d - 1], b_recv.at[z, s], dev(zz, x, c))
    for k, h in early[H:]:
        send_a(k, h)

    first = s * classes
    for i in range(classes):
        rows = pl.ds(i * ROTS, ROTS)
        base[rows, :] = jnp.full((ROTS, nb), prior_ref[first + i], jnp.float32)
        act[rows, :] = jnp.full((ROTS, nb), mask_ref[first + i], jnp.int32).astype(jnp.float32)

    tmpl_copy.wait()

    @pl.loop(0, refs // 16)
    def _(i):
        rows = pl.ds(pl.multiple_of(i * 16, 16), 16)
        t = tmpl[rows, :].astype(jnp.float32)
        tnorm[rows, :] = jnp.broadcast_to(jnp.sum(t * t, axis=1, keepdims=True), (16, nb))

    all_ids = ids_ref[...]
    all_ctf = jnp.zeros(all_ids.shape, jnp.float32)
    all_prec = all_ctf
    for i in range(ctf_ref.shape[0]):
        hit = all_ids == i
        all_ctf = jnp.where(hit, ctf_ref[i], all_ctf)
        all_prec = jnp.where(hit, prec_ref[i], all_prec)

    def chunk(row, k):
        return jnp.concatenate([row[:, q * K * r + k * r : q * K * r + (k + 1) * r] for q in range(S)], axis=1)

    ctfs = [chunk(all_ctf, k) for k in range(K)]
    precs = [chunk(all_prec, k) for k in range(K)]

    def gather(k):
        own_copies[k].wait()
        for h in range(H):
            for dx in range(1, X):
                xx, _ = xc(dx, 0)
                slot = xx * C + c
                arrive(piece(k, h, slot), a_recv.at[k, h, slot])
                for dc in range(1, C):
                    _, cc = xc(0, dc)
                    remote(piece(k, h, slot), piece(k, h, slot), f_send.at[k, h, dx - 1, dc - 1], a_recv.at[k, h, slot], dev(z, x, cc))
        for h in range(H):
            for dx in range(X):
                for dc in range(1, C):
                    xx, cc = xc(dx, dc)
                    slot = xx * C + cc
                    arrive(piece(k, h, slot), a_recv.at[k, h, slot])

    p_copies = []

    def scores(k):
        pixels = grid_buf[k].reshape(nb, pix)
        raw = lax.dot_general(tmpl[...], pixels, (((1,), (1,)), ((), ())), preferred_element_type=jnp.float32)
        ctf, prec = ctfs[k], precs[k]
        values = (prec * ctf) * raw - (0.5 * prec * ctf * ctf) * tnorm[...] + base[...]
        values = jnp.where(act[...] > 0.0, values, MASKED)
        score[k] = values
        peak = jnp.max(values, axis=0, keepdims=True)
        total = jnp.sum(jnp.where(act[...] > 0.0, jnp.exp(values - peak), 0.0), axis=0, keepdims=True)
        row = lax.broadcasted_iota(jnp.int32, (8, nb), 0)
        own_stat[k] = jnp.where(row == 0, peak, total)
        for i, (dx, dc) in enumerate(peers):
            xx, cc = xc(dx, dc)
            remote(own_stat.at[k], stat.at[k, s], s_send.at[k, i], s_recv.at[k, s], dev(z, xx, cc))
        cols = pl.ds(pl.multiple_of(z * pb, pb), pb)
        p_copies.append(local(grid_buf.at[k, :, :, cols], all_p.at[z, k], p_own.at[k]))

    def w_go(k, zz, right):
        step = 1 if right else -1
        return pltpu.make_async_remote_copy(
            src_ref=all_w.at[k, zz], dst_ref=all_w.at[k, zz], send_sem=w_out.at[0 if right else 1, k, zz],
            recv_sem=w_recv.at[k, zz], device_id=dev(lax.rem(z + step + Z, Z), x, c), device_id_type=MESH,
        )

    def weights(k):
        parts = [(own_stat[k][0:1], own_stat[k][1:2])]
        for dx, dc in peers:
            xx, cc = xc(dx, dc)
            slot = xx * C + cc
            arrive(stat.at[k, slot], s_recv.at[k, slot])
            got = stat[k, slot]
            parts.append((got[0:1], got[1:2]))
        peak = functools.reduce(jnp.maximum, [p for p, _ in parts])
        total = functools.reduce(jnp.add, [t * jnp.exp(p - peak) for p, t in parts])
        evid = peak + jnp.log(total)
        mine = evid[:, 0:r]
        for q in range(1, S):
            mine = jnp.where(s == q, evid[:, q * r : (q + 1) * r], mine)
        evid_ref[:, k * r : (k + 1) * r] = mine
        post = jnp.where(act[...] > 0.0, jnp.exp(score[k] - peak), 0.0) / total
        all_w[k, z] = (post * (precs[k] * ctfs[k])).astype(jnp.bfloat16)

        @pl.when(z < Z - 1)
        def _():
            w_go(k, z, True).start()

        @pl.when(z > 0)
        def _():
            w_go(k, z, False).start()

    gather(0)
    scores(0)
    for k in range(1, K):
        for h in range(H):
            if (k, h) not in early:
                send_a(k, h)
    for k in range(1, K):
        gather(k)
        weights(k - 1)
        scores(k)

    def b_block(zz, slot):
        return all_p.at[zz, :, slot]

    def b_forward(zz):
        out = []
        for dx in range(1, X):
            xx, cc = xc(dx, 0)
            out.append((g_send.at[zz, dx - 1, 0], dev(z, xx, cc)))
        for dc in range(1, C):
            xx, cc = xc(0, dc)
            out.append((g_send.at[zz, X - 1, dc - 1], dev(z, xx, cc)))
        return [
            pltpu.make_async_remote_copy(
                src_ref=b_block(zz, s), dst_ref=b_block(zz, s), send_sem=sem, recv_sem=b_recv.at[zz, s],
                device_id=to, device_id_type=MESH,
            )
            for sem, to in out
        ]

    def b_second(zz):
        out = []
        for dx in range(1, X):
            xx, _ = xc(dx, 0)
            slot = xx * C + c
            for dc in range(1, C):
                _, cc = xc(0, dc)
                out.append(pltpu.make_async_remote_copy(
                    src_ref=b_block(zz, slot), dst_ref=b_block(zz, slot), send_sem=g_send.at[zz, dx - 1, dc],
                    recv_sem=b_recv.at[zz, slot], device_id=dev(z, x, cc), device_id_type=MESH,
                ))
        return out

    def both(d, fn):
        @pl.when(z - d >= 0)
        def _():
            fn(z - d, True)

        @pl.when(z + d < Z)
        def _():
            fn(z + d, False)

    def b_start(zz, right):
        arrive(b_block(zz, s), b_recv.at[zz, s])
        for cp in b_forward(zz):
            cp.start()

    @pl.loop(1, Z)
    def _(d):
        both(d, b_start)

    weights(K - 1)

    def product(zz):
        w = jnp.concatenate([all_w[k, zz] for k in range(K)], axis=1)
        p = all_p[zz].reshape(K * nb, pb)
        return jnp.dot(w, p, preferred_element_type=jnp.float32)

    for cp in p_copies:
        cp.wait()
    sums_ref[...] = product(z)

    def w_step(src, right):
        for k in range(K):
            arrive(all_w.at[k, src], w_recv.at[k, src])

            @pl.when((z < Z - 1) if right else (z > 0))
            def _():
                w_go(k, src, right).start()

    def p_step(src, right):
        for dx in range(1, X):
            xx, _ = xc(dx, 0)
            arrive(b_block(src, xx * C + c), b_recv.at[src, xx * C + c])
        for cp in b_second(src):
            cp.start()

    def add_step(src, right):
        for dx in range(X):
            for dc in range(1, C):
                xx, cc = xc(dx, dc)
                arrive(b_block(src, xx * C + cc), b_recv.at[src, xx * C + cc])
        sums_ref[...] += product(src)

    @pl.loop(1, Z + 1)
    def _(d):
        both(d, w_step)
        both(d, p_step)

        @pl.when(d > 1)
        def _():
            both(d - 1, add_step)

    for cp in started:
        cp.wait_send()

    def end_step(src, right):
        for cp in b_forward(src) + b_second(src):
            cp.wait_send()

    @pl.loop(1, Z)
    def _(d):
        both(d, end_step)

    for k in range(K):
        @pl.loop(0, Z)
        def _(d):
            @pl.when((z - d >= 0) & (z < Z - 1))
            def _():
                w_go(k, z - d, True).wait_send()

            @pl.when((z + d < Z) & (z > 0))
            def _():
                w_go(k, z + d, False).wait_send()


def exchange(mesh, images, templates, group_ids, group_ctf, group_prec, log_prior, class_mask):
    Z, X, C, K = mesh.shape["img"], mesh.shape["tpl"], mesh.shape["sub"], CHUNKS
    S = X * C
    rows, pix = images.shape
    refs = templates.shape[0]
    r = rows // K
    nb = S * r
    pb = pix // Z
    H = 2 if r % 32 == 0 else 1
    smem = pl.BlockSpec(memory_space=pltpu.SMEM)
    vmem = pl.BlockSpec(memory_space=pltpu.VMEM)
    anyw = pl.BlockSpec(memory_space=pl.ANY)
    dma = pltpu.SemaphoreType.DMA
    f32, bf16 = jnp.float32, jnp.bfloat16
    class_sums, evid = pl.pallas_call(
        functools.partial(exchange_kernel, (Z, X, C, K, H)),
        out_shape=(
            jax.ShapeDtypeStruct((refs, pb), f32),
            jax.ShapeDtypeStruct((1, rows), f32),
        ),
        in_specs=[vmem, smem, smem, smem, smem, anyw, anyw],
        out_specs=(vmem, vmem),
        scratch_shapes=[
            pltpu.VMEM((K, S, r, pix), bf16),
            pltpu.VMEM((refs, pix), bf16),
            pltpu.VMEM((refs, nb), f32),
            pltpu.VMEM((refs, nb), f32),
            pltpu.VMEM((refs, nb), f32),
            pltpu.VMEM((K, refs, nb), f32),
            pltpu.VMEM((K, Z, refs, nb), bf16),
            pltpu.VMEM((Z, K, S, r, pb), bf16),
            pltpu.VMEM((K, 8, nb), f32),
            pltpu.VMEM((K, S, 8, nb), f32),
            dma(()), dma((K,)), dma((K, H, S)), dma((K, H, S)), dma((K, H, max(X - 1, 1), max(C - 1, 1))),
            dma((max(Z - 1, 1),)), dma((Z, S)), dma((Z, X, C)), dma((K, max(S - 1, 1))), dma((K, S)),
            dma((2, K, Z)), dma((K, Z)), dma((K,)),
        ],
        compiler_params=pltpu.CompilerParams(
            collective_id=0, has_side_effects=True, vmem_limit_bytes=56 * 1024 * 1024
        ),
    )(group_ids.reshape(1, S * rows), group_ctf, group_prec, log_prior, class_mask, images.reshape(K, r, pix), templates)
    return class_sums, evid.reshape(rows)


def solution(mesh):
    placed = (
        P(("groups", "img", "tpl", "sub"), None),
        P(("groups", "tpl", "sub"), None),
        P(("groups", "img")),
        P("groups"),
        P("groups"),
        P("groups"),
        P("groups"),
    )
    return jax.shard_map(
        functools.partial(exchange, mesh),
        mesh=mesh,
        in_specs=placed,
        out_specs=(P(("groups", "tpl", "sub"), "img"), P(("groups", "img", "tpl", "sub"))),
        check_vma=False,
    )
```

time: 53.8 us -> 55.1 us (1.024)
  Pallas kernels: 44.4 us -> 50.6 us
  matrix products: 4.49 us -> 0 us
  other arithmetic: 1.33 us -> 0 us
  local copies, waits for them, and re-layouts: 2.62 us -> 3.68 us
    pallas_call x1, Pallas kernels: 44.4 us -> 50.6 us  [exchange(): pl.pallas_call(functools.partial(exchange_kernel, (Z, X, C, K, H)), out_s...]
    dot_general x1 -> x0, matrix products: 4.49 us -> none  [exchange(): lax.dot_general(all_w, all_p.reshape(K * Z * nb, pb), (((1,), (0,)), ((),...]
    unnamed x0 -> x4, local copies, waits for them, and re-layouts: none -> 3.68 us
    reshape x4 -> x0, local copies, waits for them, and re-layouts: 2.09 us -> none  [the longest x2 1.41 us: exchange(): ids = group_ids.reshape(S, K, r).transpose(1, 0, 2).reshape(K, 1, nb)]
    pallas_call x1 -> x0, other arithmetic: 1.33 us -> none  [exchange(): pl.pallas_call(functools.partial(exchange_kernel, (Z, X, C, K, pb)), out_...]
where the time goes in v2:
time: 55.1 us; the launch traced here: 54.9 us
  Pallas kernels  50.6 us (92%)
  local copies, waits for them, and re-layouts  3.68 us (7%)
  between operations  0.65 us (1%)
    pallas_call x1, Pallas kernels, exchange(): pl.pallas_call(functools.partial(exchange_kernel, (Z, X, C, K, H)), out_s...  50.6 us
    unnamed x4, local copies, waits for them, and re-layouts  3.68 us

profile of v2, /device:TPU:1, one launch (start us, length us, event | category | flops | bytes accessed | tf_op | source)
XLA Modules:
  0.0 54.9 jit_solution(16247848972850809349)
XLA Ops:
  0.6 50.6 %shard_map.86 = (f32[512,1024]{1,0:T(8,128)}, f32[1,64]{1,0:T(1,128)}) custom-call(s32[1,256]{1,0:T(1,128)} %bitcast.4, f32[32]{0:T(128)} %ctf_ref.1, f32[32]{0:T(128)} %prec_ref.1, f32[128]{0:T(128)} %prior_ref.1, s32[128]{0:T(128)} %mask_ref.1, bf16[2,32,4096]{2,1,0:T(8,128)(2,1)} %bitcast.3, bf16[512,4096]{1,0:T(8,128)(2,1)} %templates.1), custom_call_target="tpu_custom_call" | custom-call | tf_op jit(solution)/shard_map/pallas_call | solution.py:331
  51.2 0.0 copy-start
  51.2 3.2 %copy.11 = f32[512,1024]{1,0:T(8,128)} copy(f32[512,1024]{1,0:T(8,128)} %get-tuple-element.8) | data formatting | bytes 4194304
  54.4 0.0 copy-done
  54.4 0.5 copy.12
Async XLA Ops:
  51.2 3.2 %copy-start = (f32[1,64]{1,0:T(1,128)S(1)}, f32[1,64]{1,0:T(1,128)}, u32[]{:S(2)}) copy-start(f32[1,64]{1,0:T(1,128)} %get-tuple-element.5) | copy-start | bytes 772

commit v3 on v2

--- a/solution.py
+++ b/solution.py
@@ -13,11 +13,11 @@
 
 
 def exchange_kernel(
-    sizes, ids_ref, ctf_ref, prec_ref, prior_ref, mask_ref, images, templates,
+    sizes, ids_in, ctf_in, prec_in, prior_in, mask_in, images, templates,
     sums_ref, evid_ref,
-    grid_buf, tmpl, tnorm, base, act, score, all_w, all_p, own_stat, stat,
+    ids_ref, ctf_ref, prec_ref, prior_ref, mask_ref, grid_buf, tmpl, tnorm, base, act, score, all_w, all_p, own_stat, stat,
     tmpl_sem, own_sem, a_send, a_recv, f_send, b_send, b_recv, g_send, s_send, s_recv,
-    w_out, w_recv, p_own,
+    w_out, w_recv, p_own, in_sem,
 ):
     Z, X, C, K, H = sizes
     S = X * C
@@ -63,6 +63,12 @@
     def arrive(dst, sem):
         pltpu.make_async_copy(dst, dst, sem).wait()
 
+    small = [
+        local(src, dst, in_sem.at[i])
+        for i, (src, dst) in enumerate((
+            (ids_in, ids_ref), (ctf_in, ctf_ref), (prec_in, prec_ref), (prior_in, prior_ref), (mask_in, mask_ref),
+        ))
+    ]
     tmpl_copy = local(templates, tmpl, tmpl_sem)
     own_copies = [local(images.at[k], grid_buf.at[k, s], own_sem.at[k]) for k in range(K)]
 
@@ -81,7 +87,7 @@
             remote(src, piece(k, h, s), a_send.at[k, h, X - 1 + dc - 1], a_recv.at[k, h, s], dev(z, xx, cc))
 
     order = [(k, h) for k in range(K) for h in range(H)]
-    early = [kh for kh in order if kh[0] == 0 or kh[1] < H - 1]
+    early = [(k, h) for k, h in order if k == 0 or h < H - 1]
     for k, h in early[:H]:
         send_a(k, h)
     for d in range(1, Z):
@@ -91,6 +97,8 @@
     for k, h in early[H:]:
         send_a(k, h)
 
+    for cp in small:
+        cp.wait()
     first = s * classes
     for i in range(classes):
         rows = pl.ds(i * ROTS, ROTS)
@@ -119,16 +127,17 @@
     ctfs = [chunk(all_ctf, k) for k in range(K)]
     precs = [chunk(all_prec, k) for k in range(K)]
 
-    def gather(k):
+    def gather(k, h):
+        for dx in range(1, X):
+            xx, _ = xc(dx, 0)
+            slot = xx * C + c
+            arrive(piece(k, h, slot), a_recv.at[k, h, slot])
+            for dc in range(1, C):
+                _, cc = xc(0, dc)
+                remote(piece(k, h, slot), piece(k, h, slot), f_send.at[k, h, dx - 1, dc - 1], a_recv.at[k, h, slot], dev(z, x, cc))
+
+    def gathered(k):
         own_copies[k].wait()
-        for h in range(H):
-            for dx in range(1, X):
-                xx, _ = xc(dx, 0)
-                slot = xx * C + c
-                arrive(piece(k, h, slot), a_recv.at[k, h, slot])
-                for dc in range(1, C):
-                    _, cc = xc(0, dc)
-                    remote(piece(k, h, slot), piece(k, h, slot), f_send.at[k, h, dx - 1, dc - 1], a_recv.at[k, h, slot], dev(z, x, cc))
         for h in range(H):
             for dx in range(X):
                 for dc in range(1, C):
@@ -188,16 +197,21 @@
         def _():
             w_go(k, z, False).start()
 
-    gather(0)
-    scores(0)
-    for k in range(1, K):
+    for k in range(K):
+        late = [h for h in range(H) if (k, h) not in early]
         for h in range(H):
-            if (k, h) not in early:
-                send_a(k, h)
-    for k in range(1, K):
-        gather(k)
-        weights(k - 1)
+            if h in late or k == 0:
+                gather(k, h)
+        gathered(k)
         scores(k)
+        if k + 1 < K:
+            for h in range(H):
+                if (k + 1, h) not in early:
+                    send_a(k + 1, h)
+            for h in range(H):
+                if (k + 1, h) in early:
+                    gather(k + 1, h)
+            weights(k)
 
     def b_block(zz, slot):
         return all_p.at[zz, :, slot]
@@ -323,7 +337,6 @@
     nb = S * r
     pb = pix // Z
     H = 2 if r % 32 == 0 else 1
-    smem = pl.BlockSpec(memory_space=pltpu.SMEM)
     vmem = pl.BlockSpec(memory_space=pltpu.VMEM)
     anyw = pl.BlockSpec(memory_space=pl.ANY)
     dma = pltpu.SemaphoreType.DMA
@@ -331,12 +344,17 @@
     class_sums, evid = pl.pallas_call(
         functools.partial(exchange_kernel, (Z, X, C, K, H)),
         out_shape=(
-            jax.ShapeDtypeStruct((refs, pb), f32),
-            jax.ShapeDtypeStruct((1, rows), f32),
+            pltpu.VMEM((refs, pb), f32),
+            pltpu.VMEM((1, rows), f32),
         ),
-        in_specs=[vmem, smem, smem, smem, smem, anyw, anyw],
+        in_specs=[anyw] * 7,
         out_specs=(vmem, vmem),
         scratch_shapes=[
+            pltpu.VMEM((1, S * rows), jnp.int32),
+            pltpu.SMEM(group_ctf.shape, f32),
+            pltpu.SMEM(group_prec.shape, f32),
+            pltpu.SMEM(log_prior.shape, f32),
+            pltpu.SMEM(class_mask.shape, jnp.int32),
             pltpu.VMEM((K, S, r, pix), bf16),
             pltpu.VMEM((refs, pix), bf16),
             pltpu.VMEM((refs, nb), f32),
@@ -349,7 +367,7 @@
             pltpu.VMEM((K, S, 8, nb), f32),
             dma(()), dma((K,)), dma((K, H, S)), dma((K, H, S)), dma((K, H, max(X - 1, 1), max(C - 1, 1))),
             dma((max(Z - 1, 1),)), dma((Z, S)), dma((Z, X, C)), dma((K, max(S - 1, 1))), dma((K, S)),
-            dma((2, K, Z)), dma((K, Z)), dma((K,)),
+            dma((2, K, Z)), dma((K, Z)), dma((K,)), dma((5,)),
         ],
         compiler_params=pltpu.CompilerParams(
             collective_id=0, has_side_effects=True, vmem_limit_bytes=56 * 1024 * 1024

time: 55.1 us -> 50.7 us (0.920)
  Pallas kernels: 50.6 us -> 48.1 us
  local copies, waits for them, and re-layouts: 3.68 us -> 1.83 us
    pallas_call x1, Pallas kernels: 50.6 us -> 48.1 us  [exchange(): pl.pallas_call(functools.partial(exchange_kernel, (Z, X, C, K, H)), out_s...]
    unnamed x4 -> x2, local copies, waits for them, and re-layouts: 3.68 us -> 1.83 us
where the time goes in v3:
time: 50.7 us; the launch traced here: 50.5 us
  Pallas kernels  48.1 us (95%)
  local copies, waits for them, and re-layouts  1.83 us (4%)
  between operations  0.64 us (1%)
    pallas_call x1, Pallas kernels, exchange(): pl.pallas_call(functools.partial(exchange_kernel, (Z, X, C, K, H)), out_s...  48.1 us
    unnamed x2, local copies, waits for them, and re-layouts  1.83 us

profile of v3, /device:TPU:1, one launch (start us, length us, event | category | flops | bytes accessed | tf_op | source)
XLA Modules:
  0.0 50.5 jit_solution(7496825908037532250)
XLA Ops:
  0.6 48.1 %shard_map.86 = (f32[512,1024]{1,0:T(8,128)S(1)}, f32[1,64]{1,0:T(1,128)S(1)}) custom-call(s32[1,256]{1,0:T(1,128)} %bitcast.5, f32[32]{0:T(128)} %ctf_in.1, f32[32]{0:T(128)} %prec_in.1, f32[128]{0:T(128)} %prior_in.1, s32[128]{0:T(128)} %mask_in.1, bf16[2,32,4096]{2,1,0:T(8,128)(2,1)} %bitcast.4, bf16[512,4096]{1,0:T(8,128)(2,1)} %templates.1), custom_call_target="tpu_custom_call" | custom-call | tf_op jit(solution)/shard_map/pallas_call | solution.py:344
  48.7 1.3 %copy.11 = f32[512,1024]{1,0:T(8,128)} copy(f32[512,1024]{1,0:T(8,128)S(1)} %get-tuple-element.6) | data formatting | bytes 4194304
  50.0 0.5 %copy.12 = f32[64]{0:T(128)} copy(f32[64]{0:T(128)S(1)} %bitcast.3) | data formatting | bytes 512

commit v4 on v3

--- a/solution.py
+++ b/solution.py
@@ -87,7 +87,7 @@
             remote(src, piece(k, h, s), a_send.at[k, h, X - 1 + dc - 1], a_recv.at[k, h, s], dev(z, xx, cc))
 
     order = [(k, h) for k in range(K) for h in range(H)]
-    early = [(k, h) for k, h in order if k == 0 or h < H - 1]
+    early = [(k, h) for k, h in order ]
     for k, h in early[:H]:
         send_a(k, h)
     for d in range(1, Z):

time: 50.7 us -> 48 us (0.947)
  Pallas kernels: 48.1 us -> 45.4 us
    pallas_call x1, Pallas kernels: 48.1 us -> 45.4 us  [exchange(): pl.pallas_call(functools.partial(exchange_kernel, (Z, X, C, K, H)), out_s...]
where the time goes in v4:
time: 48 us; the launch traced here: 47.8 us
  Pallas kernels  45.4 us (95%)
  local copies, waits for them, and re-layouts  1.83 us (4%)
  between operations  0.64 us (1%)
    pallas_call x1, Pallas kernels, exchange(): pl.pallas_call(functools.partial(exchange_kernel, (Z, X, C, K, H)), out_s...  45.4 us
    unnamed x2, local copies, waits for them, and re-layouts  1.83 us

profile of v4, /device:TPU:1, one launch (start us, length us, event | category | flops | bytes accessed | tf_op | source)
XLA Modules:
  0.0 47.8 jit_solution(13620729279689961234)
XLA Ops:
  0.6 45.4 %shard_map.86 = (f32[512,1024]{1,0:T(8,128)S(1)}, f32[1,64]{1,0:T(1,128)S(1)}) custom-call(s32[1,256]{1,0:T(1,128)} %bitcast.5, f32[32]{0:T(128)} %ctf_in.1, f32[32]{0:T(128)} %prec_in.1, f32[128]{0:T(128)} %prior_in.1, s32[128]{0:T(128)} %mask_in.1, bf16[2,32,4096]{2,1,0:T(8,128)(2,1)} %bitcast.4, bf16[512,4096]{1,0:T(8,128)(2,1)} %templates.1), custom_call_target="tpu_custom_call" | custom-call | tf_op jit(solution)/shard_map/pallas_call | solution.py:344
  46.0 1.3 %copy.11 = f32[512,1024]{1,0:T(8,128)} copy(f32[512,1024]{1,0:T(8,128)S(1)} %get-tuple-element.6) | data formatting | bytes 4194304
  47.3 0.5 %copy.12 = f32[64]{0:T(128)} copy(f32[64]{0:T(128)S(1)} %bitcast.3) | data formatting | bytes 512

commit v5 on v4

--- a/solution.py
+++ b/solution.py
@@ -259,11 +259,11 @@
         for cp in b_forward(zz):
             cp.start()
 
+    weights(K - 1)
+
     @pl.loop(1, Z)
     def _(d):
         both(d, b_start)
-
-    weights(K - 1)
 
     def product(zz):
         w = jnp.concatenate([all_w[k, zz] for k in range(K)], axis=1)

time: 48 us -> 47.9 us (level)
  no operation moved by 1% of the time
where the time goes in v5:
time: 47.9 us; the launch traced here: 47.8 us
  Pallas kernels  45.3 us (95%)
  local copies, waits for them, and re-layouts  1.83 us (4%)
  between operations  0.64 us (1%)
    pallas_call x1, Pallas kernels, exchange(): pl.pallas_call(functools.partial(exchange_kernel, (Z, X, C, K, H)), out_s...  45.3 us
    unnamed x2, local copies, waits for them, and re-layouts  1.83 us

profile of v5, /device:TPU:1, one launch (start us, length us, event | category | flops | bytes accessed | tf_op | source)
XLA Modules:
  0.0 47.8 jit_solution(838609203847837195)
XLA Ops:
  0.6 45.3 %shard_map.86 = (f32[512,1024]{1,0:T(8,128)S(1)}, f32[1,64]{1,0:T(1,128)S(1)}) custom-call(s32[1,256]{1,0:T(1,128)} %bitcast.5, f32[32]{0:T(128)} %ctf_in.1, f32[32]{0:T(128)} %prec_in.1, f32[128]{0:T(128)} %prior_in.1, s32[128]{0:T(128)} %mask_in.1, bf16[2,32,4096]{2,1,0:T(8,128)(2,1)} %bitcast.4, bf16[512,4096]{1,0:T(8,128)(2,1)} %templates.1), custom_call_target="tpu_custom_call" | custom-call | tf_op jit(solution)/shard_map/pallas_call | solution.py:344
  46.0 1.3 %copy.11 = f32[512,1024]{1,0:T(8,128)} copy(f32[512,1024]{1,0:T(8,128)S(1)} %get-tuple-element.6) | data formatting | bytes 4194304
  47.3 0.5 %copy.12 = f32[64]{0:T(128)} copy(f32[64]{0:T(128)S(1)} %bitcast.3) | data formatting | bytes 512
